TPU v7x, 256 devices: a whole 4x4x8 slice. The times are simulated.
256 devices in a mesh: ex: 16 (over y_hi, x, core), co: 16 (over y_lo, z).
Axes of the slice: x: 4, y: 4 (y_hi: 2, y_lo: 2; y = y_hi * 2 + y_lo), z: 8, core: 2. Of those that a mesh axis runs over, the one named last changes fastest.
Arguments:
- train_grads: float32 [16384, 32768], P('ex', 'co')
- queries: float32 [1024, 32768], P('ex', 'co'), may hold values from -6 to 6
- module_ids: int32 [8], replicated, may hold values from 0 to 223
- module_scale: float32 [224], replicated, may hold values from 0.3 to 3
- example_ids: int32 [16384], P('ex'), may hold values from 0 to 16383, as said below
Outputs:
- influence: float32 [1024, 16384], P('co', 'ex')
Inputs may be any that keep to these rules, and one draw needn't show every extreme that they name: `example_ids`: the examples of block s of 1024 rows carry the ids s * 1024 to (s + 1) * 1024 - 1, each once.
All inputs are finite; a program needn't handle non-finite values.
Results may differ from a plain program's by a relative error of at most 0.00008.
Values sent between devices are 32-bit elements; how exact they have to be, the bound alone decides.
No kernel may reach another device: no remote copies, remote signals or barrier semaphores. Data moves between devices by JAX's collectives and lax.ppermute only.
A program may use at most 128 MiB of HBM per device.

v0:
```python
import jax
import jax.numpy as jnp
from jax import lax
from jax.sharding import PartitionSpec as P

PROJ = 4096


epsilon = 1e-06


def total_of_pieces(x, axis):
    return lax.all_gather(x, axis).sum(0)


def score_block(query_rows, train_grads):
    return lax.dot_general(
        query_rows,
        train_grads,
        (((1,), (1,)), ((), ())),
        precision=lax.Precision.HIGHEST,
        preferred_element_type=jnp.float32,
    )


def shards(train_grads, queries, module_ids, module_scale, example_ids):
    example_count = train_grads.shape[0]
    coord_count = train_grads.shape[1]
    module_count = module_ids.shape[0]
    offset = lax.axis_index("co") * coord_count
    position = offset + lax.iota(jnp.int32, coord_count)
    table_index = lax.iota(jnp.int32, module_scale.shape[0])
    picked = jnp.sum(
        jnp.where(module_ids[:, None] == table_index[None, :], module_scale[None, :], 0.0), axis=1
    )
    window_index = lax.iota(jnp.int32, module_count)
    local_module = position // PROJ
    coord_scale = jnp.sum(
        jnp.where(local_module[:, None] == window_index[None, :], picked[None, :], 0.0), axis=1
    )
    scaled = queries * coord_scale[None, :]
    squares = jnp.sum(train_grads * train_grads, axis=1)
    norm_total = total_of_pieces(squares, "co")
    inverse_norm = lax.rsqrt(norm_total + epsilon)
    all_queries = lax.all_gather(scaled, "ex", axis=0, tiled=True)
    own_scores = lax.psum_scatter(
        score_block(all_queries, train_grads), "co", scatter_dimension=0, tiled=True
    )
    normed = own_scores * inverse_norm[None, :]
    local_ids = example_ids - lax.axis_index("ex") * example_count
    return jnp.zeros_like(normed).at[:, local_ids].set(normed)


def solution(mesh):
    return jax.shard_map(
        shards,
        mesh=mesh,
        in_specs=(P("ex", "co"), P("ex", "co"), P(), P(), P("ex")),
        out_specs=P("co", "ex"),
        check_vma=False,
    )
```

profile of v0, /device:TPU:2, one launch (start us, length us, event | category | flops | bytes accessed | tf_op | source)
XLA Modules:
  0.0 214.1 jit_solution(3390543927937948465)
XLA Ops:
  6.5 0.0 all-gather.3.cloned.1.call-start
  6.6 0.9 select_reduce_fusion.1
  7.4 0.1 select_reduce_fusion
  7.5 1.9 broadcast_multiply_fusion
  9.4 0.0 all-gather.3.cloned.1.call-update
  9.5 0.0 reduce-scatter.2.cloned.1.call-start
  9.5 80.2 %all-gather.3.cloned.1.call-done = f32[1024,2048]{1,0:T(8,128)} async-done(((f32[64,2048]{1,0:T(8,128)}), f32[1024,2048]{1,0:T(8,128)}) %all-gather.3.cloned.1.call-update) | async-done | bytes 8388624 | tf_op jit(solution)/shard_map/all_gather | solution.py:45
  89.7 32.1 %fusion.5 = f32[1024,1024]{1,0:T(8,128)} fusion(f32[1024,2048]{1,0:T(8,128)} %all-gather.3.cloned.1.call-done, f32[1024,2048]{1,0:T(8,128)} %param.5), kind=kOutput, calls=%fused_computation.21 | convolution fusion | flops 25769803776 | bytes 20971520 | tf_op jit(solution)/shard_map/dot_general | solution.py:17
  121.8 0.0 copy-start
  121.8 0.0 reduce-scatter.2.cloned.1.call-update
  121.8 4.0 %multiply_reduce_fusion = f32[1024]{0:T(1024)S(1)} fusion(f32[1024,2048]{1,0:T(8,128)} %param.5), kind=kLoop, calls=%fused_computation.1 | loop fusion | flops 4193280 | bytes 8392704 | tf_op jit(solution)/shard_map/reduce_sum | solution.py:42
  125.8 33.2 %all-gather = f32[16384]{0:T(1024)S(1)} all-gather(f32[1024]{0:T(1024)S(1)} %multiply_reduce_fusion), channel_id=2, replica_groups=mesh['ex'=16,'co'=16] {'co'}, dimensions={0}, use_global_device_ids=true | all-gather | bytes 69632 | tf_op jit(solution)/shard_map/all_gather | solution.py:13
  159.1 0.0 copy-done
  159.1 42.9 %reduce-scatter.2.cloned.1.call-done = f32[64,1024]{1,0:T(8,128)} async-done(((f32[1024,1024]{1,0:T(8,128)}), f32[64,1024]{1,0:T(8,128)}) %reduce-scatter.2.cloned.1.call-update) | async-done | bytes 262160 | tf_op jit(solution)/shard_map/reduce_scatter | solution.py:46
  202.0 1.0 multiply_bitcast_fusion
  203.0 0.2 copy.10
  203.2 3.2 %scatter_custom_fusion = f32[64,1024]{0,1:T(8,128)S(1)} fusion(s32[1024]{0:T(1024)S(1)} %compare_select_fusion, f32[1024,64]{1,0:T(8,128)S(1)} %copy.10, f32[]{:T(128)} %constant.11.clone.1), kind=kCustom, calls=%fused_computation.4 | custom fusion | bytes 262148 | tf_op jit(solution)/shard_map/scatter | solution.py:51
  206.4 0.9 copy.11
  (5 shorter events, 0.1 us)
Async XLA Ops:
  6.5 83.1 %all-gather.3.cloned.1.call-start = ((), (), s32[]{:S(2)}) async-start(), calls=%async_computation.1 | async-start | bytes 8912896 | tf_op jit(solution)/shard_map/all_gather | solution.py:45
  9.5 192.5 %reduce-scatter.2.cloned.1.call-start = ((), (), s32[]{:S(2)}) async-start(), calls=%async_computation.2 | async-start | bytes 4456448 | tf_op jit(solution)/shard_map/reduce_scatter | solution.py:46
  121.8 37.3 %copy-start = (s32[1024]{0:T(1024)S(1)}, s32[1024]{0:T(1024)}, u32[]{:S(2)}) copy-start(s32[1024]{0:T(1024)} %param.9) | copy-start | bytes 12292
Sparse Core Ops, SparseCore 0:
  10.1 79.5 all-gather.2
  121.9 80.0 reduce-scatter.1
where the time goes:
time: 214 us
  waiting for transfers between devices  123 us (57%)
  blocking collectives  33.2 us (16%)
  matrix products  32.1 us (15%)
  between operations  13.5 us (6%)
  other arithmetic  7.89 us (4%)
  local copies, waits for them, and re-layouts  4.32 us (2%)
    all_gather x1, waiting for transfers between devices, shards(): all_queries = lax.all_gather(scaled, 'ex', axis=0, tiled=True)  80.2 us
    reduce_scatter x1, waiting for transfers between devices, shards(): lax.psum_scatter(score_block(all_queries, train_grads), 'co', scatter_dim...  42.9 us
    all_gather x1, blocking collectives, total_of_pieces(): return lax.all_gather(x, axis).sum(0)  33.2 us
    dot_general x1, matrix products, score_block(): lax.dot_general(query_rows, train_grads, (((1,), (1,)), ((), ())), precis...  32.1 us
  transfers between devices with their start and end apart: 2, of which 2 were waited for; matrix products, arithmetic and copies ran while one was open for 2% of the time, Pallas kernels for 0%

commit v1 on v0

v1 whole, which is shorter than its diff:
```python
import jax
import jax.numpy as jnp
from jax import lax
from jax.sharding import PartitionSpec as P

PROJ = 4096
CHUNKS = 4
epsilon = 1e-06


def shards(train_grads, queries, module_ids, module_scale, example_ids):
    example_count, coord_count = train_grads.shape
    offset = lax.axis_index("co") * coord_count
    position = offset + lax.iota(jnp.int32, coord_count)
    table_index = lax.iota(jnp.int32, module_scale.shape[0])
    picked = jnp.sum(
        jnp.where(module_ids[:, None] == table_index[None, :], module_scale[None, :], 0.0), axis=1
    )
    window_index = lax.iota(jnp.int32, module_ids.shape[0])
    coord_scale = jnp.sum(
        jnp.where((position // PROJ)[:, None] == window_index[None, :], picked[None, :], 0.0), axis=1
    )
    scaled = queries * coord_scale[None, :]
    squares = jnp.sum(train_grads * train_grads, axis=1)
    norm_total = lax.all_gather(squares, "co").sum(0)
    inverse_norm = lax.rsqrt(norm_total + epsilon)
    rows = queries.shape[0] // CHUNKS
    outs = []
    for k in range(CHUNKS):
        all_q = lax.all_gather(scaled[k * rows:(k + 1) * rows], "ex", axis=0, tiled=True)
        s = lax.dot_general(all_q, train_grads, (((1,), (1,)), ((), ())),
                            precision=lax.Precision.HIGH, preferred_element_type=jnp.float32)
        outs.append(lax.psum_scatter(s, "co", scatter_dimension=0, tiled=True))
    own = jnp.concatenate(outs, 0)
    normed = own * inverse_norm[None, :]
    local_ids = example_ids - lax.axis_index("ex") * example_count
    return jnp.zeros_like(normed).at[:, local_ids].set(normed)


def solution(mesh):
    return jax.shard_map(shards, mesh=mesh,
        in_specs=(P("ex", "co"), P("ex", "co"), P(), P(), P("ex")),
        out_specs=P("co", "ex"), check_vma=False)
```

time: 214 us -> 527 us (2.46)
  waiting for transfers between devices: 123 us -> 433 us
    reduce_scatter x1 -> x4, waiting for transfers between devices: 42.9 us -> 237 us  [shards(): outs.append(lax.psum_scatter(s, 'co', scatter_dimension=0, tiled=True))]
    all_gather x1 -> x4, waiting for transfers between devices: 80.2 us -> 194 us  [shards(): lax.all_gather(scaled[k * rows:(k + 1) * rows], 'ex', axis=0, tiled=True)]
    dot_general x1 -> x4, matrix products: 32.1 us -> 34.5 us  [shards(): lax.dot_general(all_q, train_grads, (((1,), (1,)), ((), ())), precision=l...]
  transfers between devices with their start and end apart: 2 -> 8, of which waited for: 2 -> 8; matrix products, arithmetic and copies ran while one was open for 2% -> 7% of each run, Pallas kernels for 0% -> 0%
where the time goes in v1:
time: 527 us
  waiting for transfers between devices  433 us (82%)
  matrix products  34.5 us (7%)
  blocking collectives  33.3 us (6%)
  between operations  13.6 us (3%)
  other arithmetic  7.04 us (1%)
    reduce_scatter x4, waiting for transfers between devices, shards(): outs.append(lax.psum_scatter(s, 'co', scatter_dimension=0, tiled=True))  237 us
    all_gather x4, waiting for transfers between devices, shards(): lax.all_gather(scaled[k * rows:(k + 1) * rows], 'ex', axis=0, tiled=True)  194 us
    dot_general x4, matrix products, shards(): lax.dot_general(all_q, train_grads, (((1,), (1,)), ((), ())), precision=l...  34.5 us
    all_gather x1, blocking collectives, shards(): norm_total = lax.all_gather(squares, 'co').sum(0)  33.3 us
  transfers between devices with their start and end apart: 8, of which 8 were waited for; matrix products, arithmetic and copies ran while one was open for 7% of the time, Pallas kernels for 0%

profile of v1, /device:TPU:2, one launch (start us, length us, event | category | flops | bytes accessed | tf_op | source)
XLA Modules:
  0.0 527.2 jit_solution(14822634921270370738)
XLA Ops:
  6.6 0.9 select_reduce_fusion.1
  7.5 1.1 broadcast_multiply_fusion
  8.6 0.8 fusion.6
  9.5 0.7 all-gather.6.cloned.1.call-update
  10.2 0.7 all-gather.8.cloned.1.call-update
  11.0 0.5 all-gather.10.cloned.1.call-update
  11.5 54.8 %all-gather.12.cloned.1.call-done = f32[256,2048]{1,0:T(8,128)} async-done(((f32[16,2048]{1,0:T(8,128)}), f32[256,2048]{1,0:T(8,128)}) %all-gather.12.cloned.1.call-update) | async-done | bytes 2097168 | tf_op jit(solution)/shard_map/all_gather | solution.py:30
  66.3 8.7 %fusion.10 = f32[256,1024]{1,0:T(8,128)} fusion(f32[256,2048]{1,0:T(8,128)} %all-gather.12.cloned.1.call-done, f32[1024,2048]{1,0:T(8,128)} %param.5), kind=kOutput, calls=%fused_computation.26 | convolution fusion | flops 3221225472 | bytes 11534336 | tf_op jit(solution)/shard_map/dot_general | solution.py:31
  75.1 46.4 %all-gather.6.cloned.1.call-done = f32[256,2048]{1,0:T(8,128)} async-done(((f32[16,2048]{1,0:T(8,128)}), f32[256,2048]{1,0:T(8,128)}) %all-gather.6.cloned.1.call-update) | async-done | bytes 2097168 | tf_op jit(solution)/shard_map/all_gather | solution.py:30
  121.5 8.6 %fusion.7 = f32[256,1024]{1,0:T(8,128)} fusion(f32[256,2048]{1,0:T(8,128)} %all-gather.6.cloned.1.call-done, f32[1024,2048]{1,0:T(8,128)} %param.5), kind=kOutput, calls=%fused_computation.23 | convolution fusion | flops 3221225472 | bytes 11534336 | tf_op jit(solution)/shard_map/dot_general | solution.py:31
  130.2 46.5 %all-gather.8.cloned.1.call-done = f32[256,2048]{1,0:T(8,128)} async-done(((f32[16,2048]{1,0:T(8,128)}), f32[256,2048]{1,0:T(8,128)}) %all-gather.8.cloned.1.call-update) | async-done | bytes 2097168 | tf_op jit(solution)/shard_map/all_gather | solution.py:30
  176.6 8.6 %fusion.8 = f32[256,1024]{1,0:T(8,128)} fusion(f32[256,2048]{1,0:T(8,128)} %all-gather.8.cloned.1.call-done, f32[1024,2048]{1,0:T(8,128)} %param.5), kind=kOutput, calls=%fused_computation.24 | convolution fusion | flops 3221225472 | bytes 11534336 | tf_op jit(solution)/shard_map/dot_general | solution.py:31
  185.3 0.2 reduce-scatter.9.cloned.1.call-start
  185.5 46.1 %all-gather.10.cloned.1.call-done = f32[256,2048]{1,0:T(8,128)} async-done(((f32[16,2048]{1,0:T(8,128)}), f32[256,2048]{1,0:T(8,128)}) %all-gather.10.cloned.1.call-update) | async-done | bytes 2097168 | tf_op jit(solution)/shard_map/all_gather | solution.py:30
  231.6 8.6 %fusion.9 = f32[256,1024]{1,0:T(8,128)} fusion(f32[256,2048]{1,0:T(8,128)} %all-gather.10.cloned.1.call-done, f32[1024,2048]{1,0:T(8,128)} %param.5), kind=kOutput, calls=%fused_computation.25 | convolution fusion | flops 3221225472 | bytes 11534336 | tf_op jit(solution)/shard_map/dot_general | solution.py:31
  240.3 4.0 multiply_reduce_fusion
  244.3 33.3 %all-gather = f32[16384]{0:T(1024)S(1)} all-gather(f32[1024]{0:T(1024)S(1)} %multiply_reduce_fusion), channel_id=2, replica_groups=mesh['ex'=16,'co'=16] {'co'}, dimensions={0}, use_global_device_ids=true | all-gather | bytes 69632 | tf_op jit(solution)/shard_map/all_gather | solution.py:25
  277.7 27.0 %reduce-scatter.11.cloned.1.call-done = f32[16,1024]{1,0:T(8,128)} async-done(((f32[256,1024]{1,0:T(8,128)}), f32[16,1024]{1,0:T(8,128)}) %reduce-scatter.11.cloned.1.call-update) | async-done | bytes 65552 | tf_op jit(solution)/shard_map/reduce_scatter | solution.py:33
  304.6 70.1 %reduce-scatter.5.cloned.1.call-done = f32[16,1024]{1,0:T(8,128)} async-done(((f32[256,1024]{1,0:T(8,128)}), f32[16,1024]{1,0:T(8,128)}) %reduce-scatter.5.cloned.1.call-update) | async-done | bytes 65552 | tf_op jit(solution)/shard_map/reduce_scatter | solution.py:33
  374.8 70.1 %reduce-scatter.7.cloned.1.call-done = f32[16,1024]{1,0:T(8,128)} async-done(((f32[256,1024]{1,0:T(8,128)}), f32[16,1024]{1,0:T(8,128)}) %reduce-scatter.7.cloned.1.call-update) | async-done | bytes 65552 | tf_op jit(solution)/shard_map/reduce_scatter | solution.py:33
  444.8 70.2 %reduce-scatter.9.cloned.1.call-done = f32[16,1024]{1,0:T(8,128)} async-done(((f32[256,1024]{1,0:T(8,128)}), f32[16,1024]{1,0:T(8,128)}) %reduce-scatter.9.cloned.1.call-update) | async-done | bytes 65552 | tf_op jit(solution)/shard_map/reduce_scatter | solution.py:33
  515.1 1.0 fusion
  516.2 3.2 scatter_custom_fusion
  519.5 0.9 copy.11
  (21 shorter events, 0.7 us)
Async XLA Ops:
  6.5 59.8 %all-gather.12.cloned.1.call-start = ((), (), s32[]{:S(2)}) async-start(), calls=%async_computation.10 | async-start | bytes 2228224 | tf_op jit(solution)/shard_map/all_gather | solution.py:30
  9.4 112.0 %all-gather.6.cloned.1.call-start = ((), (), s32[]{:S(2)}) async-start(), calls=%async_computation.4 | async-start | bytes 2228224 | tf_op jit(solution)/shard_map/all_gather | solution.py:30
  10.2 166.5 %all-gather.8.cloned.1.call-start = ((), (), s32[]{:S(2)}) async-start(), calls=%async_computation.6 | async-start | bytes 2228224 | tf_op jit(solution)/shard_map/all_gather | solution.py:30
  10.9 220.7 %all-gather.10.cloned.1.call-start = ((), (), s32[]{:S(2)}) async-start(), calls=%async_computation.8 | async-start | bytes 2228224 | tf_op jit(solution)/shard_map/all_gather | solution.py:30
  11.5 293.1 %reduce-scatter.11.cloned.1.call-start = ((), (), s32[]{:S(2)}) async-start(), calls=%async_computation.11 | async-start | bytes 1114112 | tf_op jit(solution)/shard_map/reduce_scatter | solution.py:33
  75.0 299.7 %reduce-scatter.5.cloned.1.call-start = ((), (), s32[]{:S(2)}) async-start(), calls=%async_computation.5 | async-start | bytes 1114112 | tf_op jit(solution)/shard_map/reduce_scatter | solution.py:33
  130.1 314.7 %reduce-scatter.7.cloned.1.call-start = ((), (), s32[]{:S(2)}) async-start(), calls=%async_computation.7 | async-start | bytes 1114112 | tf_op jit(solution)/shard_map/reduce_scatter | solution.py:33
  185.3 329.8 %reduce-scatter.9.cloned.1.call-start = ((), (), s32[]{:S(2)}) async-start(), calls=%async_computation.9 | async-start | bytes 1114112 | tf_op jit(solution)/shard_map/reduce_scatter | solution.py:33
  240.3 37.4 %copy-start = (s32[1024]{0:T(1024)S(1)}, s32[1024]{0:T(1024)}, u32[]{:S(2)}) copy-start(s32[1024]{0:T(1024)} %param.9) | copy-start | bytes 12292
Sparse Core Ops, SparseCore 0:
  10.1 56.1 all-gather.11
  69.1 52.3 all-gather.5
  124.2 52.3 all-gather.7
  179.2 52.3 all-gather.9
  234.0 70.5 reduce-scatter.10
  307.1 67.5 reduce-scatter.4
  377.3 67.5 reduce-scatter.6
  447.5 67.5 reduce-scatter.8
